TPU v7x, 512 devices: a whole 4x4x16 slice. The times are simulated.
512 devices in a mesh: pix: 32 (over z, core), tm: 16 (over y, x).
Axes of the slice: x: 4, y: 4, z: 16, core: 2. Of those that a mesh axis runs over, the one named last changes fastest.
Arguments:
- raw_frames: bfloat16 [1024, 262144], P('tm', 'pix'), may hold values from 0.099609375 to 4
- eigen_flats: bfloat16 [16, 262144], P(None, 'pix'), may hold values from 0 to 1
- weights: float32 [1024, 16], P('tm'), may hold values from 0.02 to 1
- flat_count: int32 [1024], P('tm'), may hold values from 1 to 16
- bin_map: int32 [262144], P('pix'), may hold values from 0 to 64, as said below
Outputs:
- two_time: float32 [64, 1024, 1024], P('pix', 'tm')
Inputs may be any that keep to these rules, and one draw needn't show every extreme that they name: `bin_map`: each block of 8192 pixels (one device's tile) holds 60 to 96 pixels of every bin 1 to 64; in every draw one bin holds exactly 96 pixels in every tile.
All inputs are finite; a program needn't handle non-finite values.
Results may differ from a plain program's by a relative error of at most 0.0003.
Values may be sent and summed in bfloat16 or wider, within the bound.
No kernel may reach another device: no remote copies, remote signals or barrier semaphores. Data moves between devices by JAX's collectives and lax.ppermute only.
A program may use at most 64 MiB of HBM per device.

v0:
```python
import jax
import jax.numpy as jnp
from jax import lax
from jax.sharding import PartitionSpec as P

CAP = 96
BIN_DEV = 2


def bin_block(own_frames, local_sums, pixel_counts, portion):
    products = jnp.einsum("tsbc,usbc->btu", own_frames, portion, preferred_element_type=jnp.float32)
    other_sums = jnp.transpose(jnp.sum(portion, axis=(1, 3), dtype=jnp.float32))
    scaled = pixel_counts[:, None, None] * products
    return scaled / (local_sums[:, :, None] * other_sums[:, None, :])


def shards(raw_frames, eigen_flats, weights, flat_count, bin_map):
    frames, pixels = raw_frames.shape
    eigen_count = eigen_flats.shape[0]
    in_use = lax.broadcasted_iota(jnp.int32, (frames, eigen_count), 1) < flat_count[:, None]
    coefficients = jnp.where(in_use, weights, 0.0)
    flat_field = 0.5 + jnp.dot(
        coefficients, eigen_flats.astype(jnp.float32), precision=lax.Precision.HIGHEST
    )
    corrected = (raw_frames.astype(jnp.float32) / flat_field).astype(jnp.bfloat16)
    owners = lax.axis_size("pix")
    bin_total = BIN_DEV * owners
    labels = jnp.where(bin_map > 0, bin_map - 1, bin_total)
    ordering = jnp.argsort(labels * pixels + jnp.arange(pixels, dtype=jnp.int32))
    member = labels[:, None] == jnp.arange(bin_total, dtype=jnp.int32)[None, :]
    counts = jnp.sum(member, axis=0, dtype=jnp.int32)
    starts = jnp.cumsum(counts) - counts
    slot_index = jnp.arange(CAP, dtype=jnp.int32)
    filled = slot_index[None, :] < counts[:, None]
    source = ordering[jnp.minimum(starts[:, None] + slot_index[None, :], pixels - 1)]
    packed = jnp.where(
        filled.reshape(-1)[None, :], corrected[:, source.reshape(-1)], jnp.zeros((), jnp.bfloat16)
    )
    tallies = counts.astype(jnp.bfloat16)[None, :]
    received, tally_in = (
        lax.all_to_all(packed, "pix", split_axis=1, concat_axis=1, tiled=True),
        lax.all_to_all(tallies, "pix", split_axis=1, concat_axis=1, tiled=True),
    )
    own_frames = received.reshape(frames, owners, BIN_DEV, CAP)
    pixel_counts = jnp.sum(tally_in.astype(jnp.float32).reshape(owners, BIN_DEV), axis=0)
    local_sums = jnp.transpose(jnp.sum(own_frames, axis=(1, 3), dtype=jnp.float32))
    return bin_block(
        own_frames, local_sums, pixel_counts, lax.all_gather(own_frames, "tm", axis=0, tiled=True)
    )


def solution(mesh):
    return jax.shard_map(
        shards,
        mesh=mesh,
        in_specs=(P("tm", "pix"), P(None, "pix"), P("tm", None), P("tm"), P("pix")),
        out_specs=P("pix", "tm", None),
        check_vma=False,
    )
```

profile of v0, /device:TPU:1, one launch (start us, length us, event | category | flops | bytes accessed | tf_op | source)
XLA Modules:
  0.0 294.0 jit_solution(1987480666871033830)
XLA Ops:
  6.6 0.8 add_select_fusion
  7.4 0.3 convert_reduce_fusion.2
  7.7 0.1 lt.61
  7.8 0.1 lt.62
  8.0 0.1 copy.28
  8.1 0.1 reduce-window.8
  8.2 0.1 reduce.3
  8.5 6.8 %sort.17 = (s32[8192]{0:T(1024)}, s32[8192]{0:T(1024)S(1)}) sort(s32[8192]{0:T(1024)S(1)} %get-tuple-element.8, s32[8192]{0:T(1024)S(1)} %iota.25), dimensions={0}, to_apply=%region_2.3 | sort | flops 106496 | bytes 131072 | tf_op jit(solution)/shard_map/jit(argsort)/sort | solution.py:29
  15.3 34.3 %gather_fusion = s32[6144]{0:T(1024)S(1)} fusion(s32[8192]{0:T(1024)S(1)} %get-tuple-element.6, s32[6144]{0:T(1024)S(1)} %broadcast_clamp_fusion), kind=kCustom, calls=%fused_computation | custom fusion | bytes 73728 | tf_op jit(solution)/shard_map/gather | solution.py:35
  49.7 1.2 fusion.1
  50.9 1.1 copy.29
  52.0 22.1 %gather_fusion.1 = bf16[6144,64]{1,0:T(8,128)(2,1)} fusion(bf16[64,8192]{0,1:T(8,128)(2,1)S(1)} %copy.29, s32[6144]{0:T(1024)S(1)} %broadcast_clamp_fusion.1), kind=kCustom, calls=%fused_computation.1 | custom fusion | bytes 1597440 | tf_op jit(solution)/shard_map/gather | solution.py:37
  74.0 1.8 copy.30
  76.0 72.2 %all_to_all.12 = bf16[64,32,192]{2,0,1:T(8,128)(2,1)S(1)} all-to-all(bf16[64,32,192]{2,0,1:T(8,128)(2,1)S(1)} %broadcast_select_fusion), channel_id=1, replica_groups=mesh['pix'=32,'tm'=16] {'pix'}, dimensions={1} | all-to-all | bytes 1572864 | tf_op jit(solution)/shard_map/all_to_all | solution.py:41
  148.2 0.6 reshape.176
  148.8 1.3 copy.33
  150.1 0.1 convert_element_type.46
  150.2 15.1 %all_to_all.13 = bf16[1,32,2]{2,0,1:T(2,128)(2,1)S(1)} all-to-all(bf16[1,32,2]{2,0,1:T(2,128)(2,1)S(1)} %convert_element_type.46), channel_id=1, replica_groups=mesh['pix'=32,'tm'=16] {'pix'}, dimensions={1} | all-to-all | bytes 256 | tf_op jit(solution)/shard_map/all_to_all | solution.py:42
  165.3 0.2 convert_reduce_fusion.1
  165.5 0.1 reduce_sum.46
  165.6 0.1 reduce_sum.47
  165.8 102.4 %all-gather.2.cloned.1.call-done = bf16[1024,32,2,96]{3,0,1,2:T(8,128)(2,1)} async-done(((bf16[64,32,2,96]{3,0,1,2:T(8,128)(2,1)}), bf16[1024,32,2,96]{3,0,1,2:T(8,128)(2,1)}) %all-gather.2.cloned.1.call-update) | async-done | bytes 12582928 | tf_op jit(solution)/shard_map/all_gather | solution.py:48
  268.2 7.2 %convert_reduce_fusion = f32[1024,2]{0,1:T(2,128)S(1)} fusion(bf16[1024,32,2,96]{3,0,1,2:T(8,128)(2,1)} %all-gather.2.cloned.1.call-done), kind=kLoop, calls=%fused_computation.2 | loop fusion | flops 12580864 | bytes 12591104 | tf_op jit(solution)/shard_map/reduce_sum | solution.py:12
  275.5 11.7 %fusion.3 = f32[2,64,1024]{2,1,0:T(8,128)} fusion(bf16[1024,32,2,96]{3,0,1,2:T(8,128)(2,1)} %all-gather.2.cloned.1.call-done, f32[2,1024]{1,0:T(2,128)S(1)} %bitcast.24, f32[2,64]{1,0:T(2,128)S(1)} %bitcast.25, f32[2]{0:T(128)S(1)} %convert_reduce_fusion.3, bf16[64,32,2,96]{3,2,0,1:T(2,128)(2,1)S(1)} %reshape.176), kind=kOutput, calls=%fused_computation.11 | convolution fusion | flops 805699584 | bytes 13902344 | tf_op jit(solution)/shard_map/tsbc,usbc->btu/dot_general | solution.py:11
  (24 shorter events, 0.6 us)
Async XLA Ops:
  6.5 43.1 %copy-start = (bf16[16,8192]{1,0:T(8,128)(2,1)S(1)}, bf16[16,8192]{1,0:T(8,128)(2,1)}, u32[]{:S(2)}) copy-start(bf16[16,8192]{1,0:T(8,128)(2,1)} %param.6) | copy-start | bytes 786436
  6.5 261.7 %all-gather.2.cloned.1.call-start = ((), (), s32[]{:S(2)}) async-start(), calls=%async_computation.2 | async-start | bytes 17825792 | tf_op jit(solution)/shard_map/all_gather | solution.py:48
  15.3 34.4 %copy-start.1 = (bf16[64,8192]{1,0:T(8,128)(2,1)S(1)}, bf16[64,8192]{1,0:T(8,128)(2,1)}, u32[]{:S(2)}) copy-start(bf16[64,8192]{1,0:T(8,128)(2,1)} %param.5) | copy-start | bytes 3145732
  15.3 34.4 %copy-start.2 = (f32[64,16]{0,1:T(8,128)S(1)}, f32[64,16]{0,1:T(8,128)}, u32[]{:S(2)}) copy-start(f32[64,16]{0,1:T(8,128)} %param.7) | copy-start | bytes 12292
  15.3 34.4 %copy-start.3 = (s32[64]{0:T(128)S(1)}, s32[64]{0:T(128)}, u32[]{:S(2)}) copy-start(s32[64]{0:T(128)} %param.8) | copy-start | bytes 772
Sparse Core Ops, SparseCore 0:
  150.2 118.0 all-gather.1
where the time goes:
time: 294 us
  waiting for transfers between devices  102 us (35%)
  blocking collectives  87.3 us (30%)
  local copies, waits for them, and re-layouts  61.9 us (21%)
  other arithmetic  15.9 us (5%)
  between operations  13.6 us (5%)
  matrix products  12.9 us (4%)
    all_gather x1, waiting for transfers between devices, shards(): lax.all_gather(own_frames, 'tm', axis=0, tiled=True)  102 us
    all_to_all x1, blocking collectives, shards(): lax.all_to_all(packed, 'pix', split_axis=1, concat_axis=1, tiled=True)  72.2 us
    gather x1, local copies, waits for them, and re-layouts, shards(): ordering[jnp.minimum(starts[:, None] + slot_index[None, :], pixels - 1)]  34.3 us
    gather x2, local copies, waits for them, and re-layouts, shards(): corrected[:, source.reshape(-1)]  23.9 us
    all_to_all x1, blocking collectives, shards(): lax.all_to_all(tallies, 'pix', split_axis=1, concat_axis=1, tiled=True)  15.1 us
    dot_general x1, matrix products, bin_block(): jnp.einsum('tsbc,usbc->btu', own_frames, portion, preferred_element_type=...  11.7 us
    reduce_sum x1, other arithmetic, bin_block(): other_sums = jnp.transpose(jnp.sum(portion, axis=(1, 3), dtype=jnp.float32))  7.24 us
    sort x1, other arithmetic, shards(): jnp.argsort(labels * pixels + jnp.arange(pixels, dtype=jnp.int32))  6.77 us
  transfers between devices with their start and end apart: 1, of which 1 were waited for; matrix products, arithmetic and copies ran while one was open for 0% of the time, Pallas kernels for 0%

commit v1 on v0

--- a/solution.py
+++ b/solution.py
@@ -45,7 +45,12 @@
     pixel_counts = jnp.sum(tally_in.astype(jnp.float32).reshape(owners, BIN_DEV), axis=0)
     local_sums = jnp.transpose(jnp.sum(own_frames, axis=(1, 3), dtype=jnp.float32))
     return bin_block(
-        own_frames, local_sums, pixel_counts, lax.all_gather(own_frames, "tm", axis=0, tiled=True)
+        own_frames,
+        local_sums,
+        pixel_counts,
+        jnp.concatenate(
+            lax.all_to_all(jnp.stack(lax.axis_size("tm") * [own_frames], 0), "tm", 0, 0), 0
+        ),
     )
 
 

time: 294 us -> 442 us (1.50)
  waiting for transfers between devices: 102 us -> 312 us
  blocking collectives: 87.3 us -> 0 us
  starting transfers between devices: 0.01 us -> 27.6 us
  between operations: 13.6 us -> 0.22 us
  local copies, waits for them, and re-layouts: 61.9 us -> 68.9 us
    all_to_all x0 -> x3, waiting for transfers between devices: none -> 312 us  [the longest x1 247 us: shards(): lax.all_to_all(jnp.stack(lax.axis_size('tm') * [own_frames], 0), 'tm', 0, 0)]
    all_gather x1 -> x0, waiting for transfers between devices: 102 us -> none  [shards(): lax.all_gather(own_frames, 'tm', axis=0, tiled=True)]
    all_to_all x2 -> x0, blocking collectives: 87.3 us -> none  [the longest x1 72.2 us: shards(): lax.all_to_all(packed, 'pix', split_axis=1, concat_axis=1, tiled=True)]
    all_to_all x0 -> x3, starting transfers between devices: none -> 27.6 us  [the longest x1 16.7 us: shards(): lax.all_to_all(packed, 'pix', split_axis=1, concat_axis=1, tiled=True)]
    another operation x1 -> x2, local copies, waits for them, and re-layouts: 0.1 us -> 6.31 us  [the longest x1 6.21 us: shards(): jnp.stack(lax.axis_size('tm') * [own_frames], 0)]
  transfers between devices with their start and end apart: 1 -> 3, of which waited for: 1 -> 3; matrix products, arithmetic and copies ran while one was open for 0% -> 1% of each run, Pallas kernels for 0% -> 0%
where the time goes in v1:
time: 442 us
  waiting for transfers between devices  312 us (71%)
  local copies, waits for them, and re-layouts  68.9 us (16%)
  starting transfers between devices  27.6 us (6%)
  other arithmetic  17.7 us (4%)
  matrix products  15.1 us (3%)
    all_to_all x1, waiting for transfers between devices, shards(): lax.all_to_all(jnp.stack(lax.axis_size('tm') * [own_frames], 0), 'tm', 0, 0)  247 us
    all_to_all x1, waiting for transfers between devices, shards(): lax.all_to_all(packed, 'pix', split_axis=1, concat_axis=1, tiled=True)  55 us
    gather x1, local copies, waits for them, and re-layouts, shards(): ordering[jnp.minimum(starts[:, None] + slot_index[None, :], pixels - 1)]  34.3 us
    gather x2, local copies, waits for them, and re-layouts, shards(): corrected[:, source.reshape(-1)]  23.9 us
    all_to_all x1, starting transfers between devices, shards(): lax.all_to_all(packed, 'pix', split_axis=1, concat_axis=1, tiled=True)  16.7 us
    dot_general x1, matrix products, bin_block(): jnp.einsum('tsbc,usbc->btu', own_frames, portion, preferred_element_type=...  13.9 us
    all_to_all x1, waiting for transfers between devices, shards(): lax.all_to_all(tallies, 'pix', split_axis=1, concat_axis=1, tiled=True)  9.98 us
  transfers between devices with their start and end apart: 3, of which 3 were waited for; matrix products, arithmetic and copies ran while one was open for 1% of the time, Pallas kernels for 0%

profile of v1, /device:TPU:1, one launch (start us, length us, event | category | flops | bytes accessed | tf_op | source)
XLA Modules:
  0.0 442.0 jit_solution(8283958780587698102)
XLA Ops:
  0.1 0.8 add_select_fusion
  0.9 0.3 convert_reduce_fusion.2
  2.0 6.8 %sort.17 = (s32[8192]{0:T(1024)}, s32[8192]{0:T(1024)S(1)}) sort(s32[8192]{0:T(1024)S(1)} %get-tuple-element.8, s32[8192]{0:T(1024)S(1)} %iota.25), dimensions={0}, to_apply=%region_2.3 | sort | flops 106496 | bytes 131072 | tf_op jit(solution)/shard_map/jit(argsort)/sort | solution.py:29
  8.8 34.3 %gather_fusion = s32[6144]{0:T(1024)S(1)} fusion(s32[8192]{0:T(1024)S(1)} %get-tuple-element.6, s32[6144]{0:T(1024)S(1)} %broadcast_clamp_fusion), kind=kCustom, calls=%fused_computation | custom fusion | bytes 73728 | tf_op jit(solution)/shard_map/gather | solution.py:35
  43.1 1.2 fusion.3
  44.3 1.1 copy.35
  45.4 22.1 %gather_fusion.1 = bf16[6144,64]{1,0:T(8,128)(2,1)} fusion(bf16[64,8192]{0,1:T(8,128)(2,1)S(1)} %copy.35, s32[6144]{0:T(1024)S(1)} %broadcast_clamp_fusion.1), kind=kCustom, calls=%fused_computation.1 | custom fusion | bytes 1597440 | tf_op jit(solution)/shard_map/gather | solution.py:37
  67.5 1.8 copy.36
  69.3 1.1 broadcast_select_fusion
  70.4 16.7 %all-to-all-start.1 = ((bf16[64,32,192]{2,0,1:T(8,128)(2,1)}), bf16[64,32,192]{2,0,1:T(8,128)(2,1)S(1)}, u32[]{:S(2)}, u32[]{:S(2)}) async-start(bf16[64,32,192]{2,0,1:T(8,128)(2,1)} %broadcast_select_fusion), calls=%async_computation.1 | async-start | bytes 2097152 | tf_op jit(solution)/shard_map/all_to_all | solution.py:41
  87.1 0.7 convert_element_type.47
  87.9 55.0 %all-to-all-done.1 = bf16[64,32,192]{2,0,1:T(8,128)(2,1)S(1)} async-done(((bf16[64,32,192]{2,0,1:T(8,128)(2,1)}), bf16[64,32,192]{2,0,1:T(8,128)(2,1)S(1)}, u32[]{:S(2)}, u32[]{:S(2)}) %all-to-all-start.1) | async-done | bytes 786464 | tf_op jit(solution)/shard_map/all_to_all | solution.py:41
  142.8 4.0 all-to-all-start
  146.9 0.6 reshape.184
  147.5 1.2 copy.38
  148.7 10.0 %all-to-all-done = bf16[1,32,2]{2,0,1:T(2,128)(2,1)S(1)} async-done(((bf16[1,32,2]{2,0,1:T(2,128)(2,1)}), bf16[1,32,2]{2,0,1:T(2,128)(2,1)S(1)}, u32[]{:S(2)}, u32[]{:S(2)}) %all-to-all-start) | async-done | bytes 160 | tf_op jit(solution)/shard_map/all_to_all | solution.py:42
  158.7 6.2 %stack.3 = bf16[16,64,32,2,96]{4,2,3,1,0:T(8,128)(2,1)} broadcast(bf16[64,32,2,96]{3,1,2,0:T(8,128)(2,1)S(1)} %copy.38), dimensions={1,2,3,4} | broadcast | bytes 13369344 | tf_op jit(solution)/shard_map/stack | solution.py:52
  164.9 6.8 %all-to-all-start.2 = ((bf16[16,64,32,2,96]{4,2,3,1,0:T(8,128)(2,1)}), bf16[16,64,32,2,96]{4,2,3,1,0:T(8,128)(2,1)}, u32[]{:S(2)}, u32[]{:S(2)}) async-start(bf16[16,64,32,2,96]{4,2,3,1,0:T(8,128)(2,1)} %stack.3), calls=%async_computation.2 | async-start | bytes 33554432 | tf_op jit(solution)/shard_map/all_to_all | solution.py:52
  171.8 0.2 convert_reduce_fusion.1
  172.1 0.1 reduce_sum.49
  172.3 247.5 %all-to-all-done.2 = bf16[16,64,32,2,96]{4,2,3,1,0:T(8,128)(2,1)} async-done(((bf16[16,64,32,2,96]{4,2,3,1,0:T(8,128)(2,1)}), bf16[16,64,32,2,96]{4,2,3,1,0:T(8,128)(2,1)}, u32[]{:S(2)}, u32[]{:S(2)}) %all-to-all-start.2) | async-done | bytes 12582944 | tf_op jit(solution)/shard_map/all_to_all | solution.py:52
  419.8 8.1 %convert_reduce_fusion = f32[16,64,2]{2,1,0:T(8,128)S(1)} fusion(bf16[16,64,32,2,96]{4,2,3,1,0:T(8,128)(2,1)} %all-to-all-done.2), kind=kLoop, calls=%fused_computation.2 | loop fusion | flops 12580864 | bytes 12591104 | tf_op jit(solution)/shard_map/reduce_sum | solution.py:12
  427.9 0.2 copy.42
  428.1 13.9 %fusion.10 = f32[2,64,1024]{2,1,0:T(8,128)} fusion(bf16[1024,32,2,96]{3,1,2,0:T(8,128)(2,1)} %bitcast.5, bf16[64,32,2,96]{3,2,0,1:T(2,128)(2,1)S(1)} %reshape.184, f32[2,1024]{1,0:T(2,128)S(1)} %bitcast.26, f32[2,64]{1,0:T(2,128)S(1)} %bitcast.28, f32[2]{0:T(128)S(1)} %convert_reduce_fusion.3), kind=kOutput, calls=%fused_computation.13 | convolution fusion | flops 805699584 | bytes 13902344 | tf_op jit(solution)/shard_map/tsbc,usbc->btu/dot_general | solution.py:11
  (27 shorter events, 1.1 us)
Async XLA Ops:
  0.0 43.1 %copy-start = (bf16[16,8192]{1,0:T(8,128)(2,1)S(1)}, bf16[16,8192]{1,0:T(8,128)(2,1)}, u32[]{:S(2)}) copy-start(bf16[16,8192]{1,0:T(8,128)(2,1)} %param.6) | copy-start | bytes 786436
  8.8 34.4 %copy-start.1 = (bf16[64,8192]{1,0:T(8,128)(2,1)S(1)}, bf16[64,8192]{1,0:T(8,128)(2,1)}, u32[]{:S(2)}) copy-start(bf16[64,8192]{1,0:T(8,128)(2,1)} %param.5) | copy-start | bytes 3145732
  8.8 34.4 %copy-start.2 = (f32[64,16]{0,1:T(8,128)S(1)}, f32[64,16]{0,1:T(8,128)}, u32[]{:S(2)}) copy-start(f32[64,16]{0,1:T(8,128)} %param.7) | copy-start | bytes 12292
  8.8 34.4 %copy-start.3 = (s32[64]{0:T(128)S(1)}, s32[64]{0:T(128)}, u32[]{:S(2)}) copy-start(s32[64]{0:T(128)} %param.8) | copy-start | bytes 772
  70.4 72.5 %all-to-all-start.1 = ((bf16[64,32,192]{2,0,1:T(8,128)(2,1)}), bf16[64,32,192]{2,0,1:T(8,128)(2,1)S(1)}, u32[]{:S(2)}, u32[]{:S(2)}) async-start(bf16[64,32,192]{2,0,1:T(8,128)(2,1)} %broadcast_select_fusion), calls=%async_computation.1 | async-start | bytes 2097152 | tf_op jit(solution)/shard_map/all_to_all | solution.py:41
  142.8 15.8 %all-to-all-start = ((bf16[1,32,2]{2,0,1:T(2,128)(2,1)}), bf16[1,32,2]{2,0,1:T(2,128)(2,1)S(1)}, u32[]{:S(2)}, u32[]{:S(2)}) async-start(bf16[1,32,2]{2,0,1:T(2,128)(2,1)} %convert_element_type.47), calls=%async_computation | async-start | bytes 32768 | tf_op jit(solution)/shard_map/all_to_all | solution.py:42
  164.9 254.9 %all-to-all-start.2 = ((bf16[16,64,32,2,96]{4,2,3,1,0:T(8,128)(2,1)}), bf16[16,64,32,2,96]{4,2,3,1,0:T(8,128)(2,1)}, u32[]{:S(2)}, u32[]{:S(2)}) async-start(bf16[16,64,32,2,96]{4,2,3,1,0:T(8,128)(2,1)} %stack.3), calls=%async_computation.2 | async-start | bytes 33554432 | tf_op jit(solution)/shard_map/all_to_all | solution.py:52
